TPU v7x, 256 devices: a whole 4x4x8 slice. The times are simulated.
256 devices in a mesh: expert: 64 (over y, z, core), tensor: 4 (over x).
Axes of the slice: x: 4, y: 4, z: 8, core: 2. Of those that a mesh axis runs over, the one named last changes fastest.
Arguments:
- attn_heads: bfloat16 [8192, 4096], P('expert', 'tensor'), may hold values from -6 to 6
- out_proj: bfloat16 [4096, 4096], P('tensor', 'expert'), may hold values from -0.09375 to 0.09375
- residual: bfloat16 [8192, 4096], P('expert'), may hold values from -6 to 6
- norm_gain: float32 [4096], replicated, may hold values from 0.1 to 1.9
- route_ids: int32 [8192, 8], P('expert'), may hold values from 0 to 63, all different within a row; in each aligned block of 128 rows (0 to 127, 128 to 255, ...) at most 18 rows name the same one
- route_weights: float32 [8192, 8], P('expert'), may hold values from 0.05 to 1
- w_gate: bfloat16 [64, 4096, 1536], P('expert', None, 'tensor'), may hold values from -0.09375 to 0.09375
- w_up: bfloat16 [64, 4096, 1536], P('expert', None, 'tensor'), may hold values from -0.09375 to 0.09375
- w_down: bfloat16 [64, 1536, 4096], P('expert', 'tensor'), may hold values from -0.15625 to 0.15625
Outputs:
- layer_out: bfloat16 [8192, 4096], P('expert', 'tensor')
Inputs may be any that keep to these rules, and one draw needn't show every extreme that they name: `route_ids`: each row names 8 different experts. In aligned blocks of 128 rows no expert is named more than 18 times, a bound that some block reaches.
All inputs are finite; a program needn't handle non-finite values.
Results may differ from a plain program's by a relative error of at most 0.015.
Values may be sent and summed in bfloat16 or wider, within the bound.
A program may use at most 128 MiB of HBM per device.

v0:
```python
import jax
import jax.numpy as jnp
from jax import lax
from jax.sharding import PartitionSpec as P

EXPERTS = 64
CAP = 18


def slot_places(ids, experts, capacity):
    row_count, top_count = ids.shape
    onehot = (ids[:, :, None] == jnp.arange(experts, dtype=jnp.int32)[None, None, :]).astype(
        jnp.int32
    )
    flattened = onehot.reshape(row_count * top_count, experts)
    before = jnp.cumsum(flattened, axis=0) - flattened
    slot_rank = jnp.sum(before * flattened, axis=1).reshape(row_count, top_count)
    return ids * capacity + slot_rank


def per_device(
    attn_heads, out_proj, residual, norm_gain, route_ids, route_weights, w_gate, w_up, w_down
):
    model_width = residual.shape[1]
    groups = lax.axis_size("expert")
    members = lax.axis_size("tensor")
    member = lax.axis_index("tensor")
    per_group = w_gate.shape[0]
    slot_count = EXPERTS * CAP
    block_cols = model_width // members
    heads_out = jnp.dot(
        attn_heads,
        lax.all_gather(out_proj, "expert", axis=1, tiled=True),
        preferred_element_type=jnp.float32,
    )
    attn_out = lax.psum(heads_out.astype(jnp.bfloat16), "tensor").astype(jnp.float32)
    hidden = residual.astype(jnp.float32) + attn_out
    normed = (
        hidden * lax.rsqrt(jnp.mean(hidden * hidden, axis=-1, keepdims=True) + 1e-06) * norm_gain
    ).astype(jnp.bfloat16)
    slot_index = slot_places(route_ids, EXPERTS, CAP)
    slot_range = jnp.arange(slot_count, dtype=jnp.int32)
    slot_hits = jnp.sum(
        (slot_index[:, :, None] == slot_range[None, None, :]).astype(jnp.bfloat16), axis=1
    )
    buffer = jnp.einsum("rj,rd->jd", slot_hits, normed, preferred_element_type=jnp.float32).astype(
        jnp.bfloat16
    )
    buffer = buffer.reshape(groups, per_group, CAP, model_width)
    arrived = lax.all_to_all(buffer, "expert", split_axis=0, concat_axis=0, tiled=True)
    gate_acc = jnp.einsum("gxcd,xdf->gxcf", arrived, w_gate, preferred_element_type=jnp.float32)
    upper = jnp.einsum("gxcd,xdf->gxcf", arrived, w_up, preferred_element_type=jnp.float32)
    activation = (jax.nn.silu(gate_acc) * upper).astype(jnp.bfloat16)
    product_term = jnp.einsum(
        "gxcf,xfd->gxcd", activation, w_down, preferred_element_type=jnp.float32
    )
    product_term = lax.optimization_barrier(product_term.astype(jnp.bfloat16)).astype(jnp.float32)
    product_term = product_term.reshape(
        groups, per_group, CAP, 1 * lax.axis_size("tensor"), block_cols
    )
    shares = lax.psum_scatter(
        jnp.transpose(product_term, (3, 0, 1, 2, 4)).astype(jnp.bfloat16),
        "tensor",
        scatter_dimension=0,
        tiled=True,
    ).astype(jnp.float32)
    expert_out = shares[0].astype(jnp.bfloat16)
    returned = lax.all_to_all(expert_out, "expert", split_axis=0, concat_axis=0, tiled=True)
    weights = route_weights / jnp.sum(route_weights, axis=-1, keepdims=True)
    picked = returned.reshape(slot_count, block_cols)[slot_index]
    mixture = jnp.sum(weights[:, :, None] * picked.astype(jnp.float32), axis=1)
    own_hidden = lax.dynamic_slice_in_dim(hidden, member * block_cols, block_cols, 1)
    return (own_hidden + mixture).astype(jnp.bfloat16)


def solution(mesh):
    placed = (
        P("expert", "tensor"),
        P("tensor", "expert"),
        P("expert", None),
        P(),
        P("expert", None),
        P("expert", None),
        P("expert", None, "tensor"),
        P("expert", None, "tensor"),
        P("expert", "tensor", None),
    )
    return jax.shard_map(
        per_device, mesh=mesh, in_specs=placed, out_specs=P("expert", "tensor"), check_vma=False
    )
```

profile of v0, /device:TPU:1, one launch (start us, length us, event | category | flops | bytes accessed | tf_op | source)
XLA Modules:
  0.0 692.8 jit_solution(6831662103066266211)
XLA Ops:
  6.5 0.7 all-gather.2.cloned.1.call-update
  7.3 90.2 %all-gather.2.cloned.1.call-done = bf16[1024,4096]{0,1:T(8,128)(2,1)} async-done(((bf16[1024,64]{0,1:T(8,128)(2,1)}), bf16[1024,4096]{0,1:T(8,128)(2,1)}) %all-gather.2.cloned.1.call-update) | async-done | bytes 8388624 | tf_op jit(solution)/shard_map/all_gather | solution.py:33
  97.5 7.4 %convolution_convert_fusion.1 = bf16[128,4096]{1,0:T(8,128)(2,1)} fusion(bf16[128,1024]{1,0:T(8,128)(2,1)} %param.9, bf16[1024,4096]{0,1:T(8,128)(2,1)} %all-gather.2.cloned.1.call-done), kind=kOutput, calls=%fused_computation.10 | convolution fusion | flops 1074266112 | bytes 9699328 | tf_op jit(solution)/shard_map/dot_general | solution.py:31
  105.0 0.1 copy.47
  105.1 0.1 eq.43
  105.3 0.7 fusion.30
  106.0 31.1 %reduce-window.6 = s32[64,8,128]{2,1,0:T(8,128)S(1)} reduce-window(s32[64,8,128]{2,1,0:T(8,128)} %fusion.30, s32[]{:T(128)} %constant.11.clone.1), window={size=1x1x128 pad=0_0x0_0x127_0}, to_apply=%region_2.0 | reduce-window | flops 8323072 | bytes 524292 | tf_op jit(solution)/shard_map/reduce-window
  137.1 0.8 slice.10
  138.0 1.1 copy.49
  139.2 0.1 broadcast_add_fusion
  139.5 0.1 copy.52
  139.7 1.5 fusion.11
  141.1 10.4 %all-reduce.2.cloned.1.call-done = bf16[128,4096]{1,0:T(8,128)(2,1)} async-done(((bf16[128,4096]{1,0:T(8,128)(2,1)}), bf16[128,4096]{1,0:T(8,128)(2,1)}) %all-reduce.2.cloned.1.call-update) | async-done | bytes 1048592 | tf_op jit(solution)/shard_map/psum | solution.py:36
  151.5 3.4 convert_add_fusion
  155.0 5.1 convolution_convert_fusion
  160.1 13.9 %reshape.76 = bf16[64,1,18,4096]{3,2,0,1:T(8,128)(2,1)} reshape(bf16[1152,4096]{1,0:T(8,128)(2,1)} %convolution_convert_fusion) | data formatting | bytes 18874368 | tf_op jit(solution)/shard_map/reshape | solution.py:49
  174.0 288.3 %all_to_all.10 = bf16[64,1,18,4096]{3,2,1,0:T(8,128)(2,1)S(1)} all-to-all(bf16[64,1,18,4096]{3,2,1,0:T(8,128)(2,1)} %bitcast.96), channel_id=1, replica_groups=mesh['expert'=64,'tensor'=4] {'expert'}, dimensions={0} | all-to-all | bytes 18874368 | tf_op jit(solution)/shard_map/all_to_all | solution.py:50
  462.3 6.2 fusion.2
  468.5 7.3 %fusion.20 = bf16[64,18,384]{2,0,1:T(8,128)(2,1)S(1)} fusion(bf16[1,4096,384]{2,1,0:T(8,128)(2,1)S(1)} %copy-done.7, bf16[64,1,18,4096]{3,2,1,0:T(8,128)(2,1)S(1)} %all_to_all.10, f32[64,18,384]{2,0,1:T(8,128)S(1)} %fusion.2), kind=kOutput, calls=%fused_computation.29 | convolution fusion | flops 3626532864 | bytes 15237120 | tf_op jit(solution)/shard_map/gxcd,xdf->gxcf/dot_general | solution.py:52
  475.9 7.5 %convert_bitcast_fusion = bf16[64,1,18,4096]{3,0,2,1:T(8,128)(2,1)} fusion(bf16[64,18,384]{2,0,1:T(8,128)(2,1)S(1)} %fusion.20, bf16[1,384,4096]{2,1,0:T(8,128)(2,1)S(1)} %copy-done), kind=kOutput, calls=%fused_computation.7 | convolution fusion | flops 3628597248 | bytes 13467648 | tf_op jit(solution)/shard_map/gxcf,xfd->gxcd/dot_general | solution.py:54
  483.3 9.0 %copy.74 = bf16[1,18,8,4,8,1024]{5,4,2,1,0,3:T(8,128)(2,1)} copy(bf16[1,18,8,4,8,1024]{5,4,3,2,1,0:T(8,128)(2,1)} %bitcast.98) | data formatting | bytes 18874368 | tf_op jit(solution)/shard_map/convert_element_type | solution.py:62
  492.3 87.7 %reduce-scatter.2.cloned.1.call-done = bf16[1,64,1,18,1024]{4,1,3,2,0:T(8,128)(2,1)} async-done(((bf16[4,64,1,18,1024]{4,1,3,2,0:T(8,128)(2,1)}), bf16[1,64,1,18,1024]{4,1,3,2,0:T(8,128)(2,1)}) %reduce-scatter.2.cloned.1.call-update) | async-done | bytes 2359312 | tf_op jit(solution)/shard_map/reduce_scatter | solution.py:61
  580.1 4.7 copy.56
  584.8 10.9 %all-to-all-start.1 = ((bf16[64,1,18,1024]{3,2,1,0:T(8,128)(2,1)}), bf16[64,1,18,1024]{3,2,1,0:T(8,128)(2,1)}, u32[]{:S(2)}, u32[]{:S(2)}) async-start(bf16[64,1,18,1024]{3,2,1,0:T(8,128)(2,1)} %copy.56), calls=%async_computation.2 | async-start | bytes 6291456 | tf_op jit(solution)/shard_map/all_to_all | solution.py:68
  595.8 0.1 copy.57
  595.9 0.1 reshape.85
  596.0 0.1 copy.46
  596.1 73.1 %all-to-all-done.1 = bf16[64,1,18,1024]{3,2,1,0:T(8,128)(2,1)} async-done(((bf16[64,1,18,1024]{3,2,1,0:T(8,128)(2,1)}), bf16[64,1,18,1024]{3,2,1,0:T(8,128)(2,1)}, u32[]{:S(2)}, u32[]{:S(2)}) %all-to-all-start.1) | async-done | bytes 2359328 | tf_op jit(solution)/shard_map/all_to_all | solution.py:68
  669.2 4.3 reshape.82
  673.5 8.0 %gather_fusion = bf16[1024,1024]{1,0:T(8,128)(2,1)} fusion(bf16[1152,1024]{1,0:T(8,128)(2,1)} %reshape.82, s32[1024]{0:T(1024)S(1)} %broadcast_clamp_fusion), kind=kCustom, calls=%fused_computation | custom fusion | bytes 4198400 | tf_op jit(solution)/shard_map/gather | solution.py:70
  681.5 2.9 fusion.7
  684.4 1.8 add_convert_fusion
  (33 shorter events, 0.6 us)
Async XLA Ops:
  6.5 469.3 %copy-start = (bf16[1,384,4096]{2,1,0:T(8,128)(2,1)S(1)}, bf16[1,384,4096]{2,1,0:T(8,128)(2,1)}, u32[]{:S(2)}) copy-start(bf16[1,384,4096]{2,1,0:T(8,128)(2,1)} %param.17) | copy-start | bytes 9437188
  6.5 90.9 %all-gather.2.cloned.1.call-start = ((), (), s32[]{:S(2)}) async-start(), calls=%async_computation.3 | async-start | bytes 8519680 | tf_op jit(solution)/shard_map/all_gather | solution.py:33
  7.3 97.7 %copy-start.4 = (s32[128,8]{0,1:T(8,128)S(1)}, s32[128,8]{0,1:T(8,128)}, u32[]{:S(2)}) copy-start(s32[128,8]{0,1:T(8,128)} %param.13) | copy-start | bytes 12292
  7.3 144.2 %all-reduce.2.cloned.1.call-start = ((), (), s32[]{:S(2)}) async-start(), calls=%async_computation.4 | async-start | bytes 2097152 | tf_op jit(solution)/shard_map/psum | solution.py:36
  104.9 475.1 %reduce-scatter.2.cloned.1.call-start = ((), (), s32[]{:S(2)}) async-start(), calls=%async_computation.5 | async-start | bytes 11796480 | tf_op jit(solution)/shard_map/reduce_scatter | solution.py:61
  137.1 17.8 %copy-start.5 = (f32[4096]{0:T(1024)S(1)}, f32[4096]{0:T(1024)}, u32[]{:S(2)}) copy-start(f32[4096]{0:T(1024)} %param.12) | copy-start | bytes 49156
  151.5 3.4 copy-start.1
  151.5 3.4 copy-start.2
  174.0 288.3 %copy-start.6 = (bf16[1,4096,384]{2,1,0:T(8,128)(2,1)S(1)}, bf16[1,4096,384]{2,1,0:T(8,128)(2,1)}, u32[]{:S(2)}) copy-start(bf16[1,4096,384]{2,1,0:T(8,128)(2,1)} %param.15) | copy-start | bytes 9437188
  462.3 6.2 copy-start.7
  584.8 11.2 %copy-start.3 = (f32[128,8]{0,1:T(8,128)S(1)}, f32[128,8]{0,1:T(8,128)}, u32[]{:S(2)}) copy-start(f32[128,8]{0,1:T(8,128)} %param.14) | copy-start | bytes 12292
  584.8 84.4 %all-to-all-start.1 = ((bf16[64,1,18,1024]{3,2,1,0:T(8,128)(2,1)}), bf16[64,1,18,1024]{3,2,1,0:T(8,128)(2,1)}, u32[]{:S(2)}, u32[]{:S(2)}) async-start(bf16[64,1,18,1024]{3,2,1,0:T(8,128)(2,1)} %copy.56), calls=%async_computation.2 | async-start | bytes 6291456 | tf_op jit(solution)/shard_map/all_to_all | solution.py:68
Sparse Core Ops, SparseCore 0:
  10.1 87.2 all-gather.1
  105.1 46.4 all-reduce.1
  492.4 87.5 reduce-scatter.1
where the time goes:
time: 695 us; the launch traced here: 693 us
  blocking collectives  288 us (41%)
  waiting for transfers between devices  262 us (38%)
  local copies, waits for them, and re-layouts  42.8 us (6%)
  other arithmetic  41.7 us (6%)
  matrix products  33.6 us (5%)
  between operations  13.3 us (2%)
  starting transfers between devices  11 us (2%)
    all_to_all x1, blocking collectives, per_device(): lax.all_to_all(buffer, 'expert', split_axis=0, concat_axis=0, tiled=True)  288 us
    all_gather x1, waiting for transfers between devices, per_device(): lax.all_gather(out_proj, 'expert', axis=1, tiled=True)  90.2 us
    reduce_scatter x1, waiting for transfers between devices, per_device(): lax.psum_scatter(jnp.transpose(product_term, (3, 0, 1, 2, 4)).astype(jnp....  87.7 us
    all_to_all x1, waiting for transfers between devices, per_device(): lax.all_to_all(expert_out, 'expert', split_axis=0, concat_axis=0, tiled=T...  73.1 us
    another operation x3, other arithmetic  31.3 us
    reshape x1, local copies, waits for them, and re-layouts, per_device(): buffer = buffer.reshape(groups, per_group, CAP, model_width)  13.9 us
  transfers between devices with their start and end apart: 4, of which 4 were waited for; matrix products, arithmetic and copies ran while one was open for 5% of the time, Pallas kernels for 0%

commit v1 on v0

--- a/solution.py
+++ b/solution.py
@@ -30,7 +30,9 @@
     block_cols = model_width // members
     heads_out = jnp.dot(
         attn_heads,
-        lax.all_gather(out_proj, "expert", axis=1, tiled=True),
+        jnp.concatenate(
+            lax.all_to_all(jnp.stack([out_proj] * lax.axis_size("expert")), "expert", 0, 0), axis=1
+        ),
         preferred_element_type=jnp.float32,
     )
     attn_out = lax.psum(heads_out.astype(jnp.bfloat16), "tensor").astype(jnp.float32)

time: 695 us -> 802 us (1.15)
  blocking collectives: 288 us -> 487 us
  waiting for transfers between devices: 262 us -> 171 us
    all_to_all x0 -> x1, blocking collectives: none -> 199 us  [per_device(): lax.all_to_all(jnp.stack([out_proj] * lax.axis_size('expert')), 'expert',...]
    all_gather x1 -> x0, waiting for transfers between devices: 90.2 us -> none  [per_device(): lax.all_gather(out_proj, 'expert', axis=1, tiled=True)]
  transfers between devices with their start and end apart: 4 -> 3, of which waited for: 4 -> 3; matrix products, arithmetic and copies ran while one was open for 5% -> 5% of each run, Pallas kernels for 0% -> 0%
where the time goes in v1:
time: 802 us; the launch traced here: 799 us
  blocking collectives  487 us (61%)
  waiting for transfers between devices  171 us (21%)
  local copies, waits for them, and re-layouts  44.9 us (6%)
  other arithmetic  41.7 us (5%)
  matrix products  30 us (4%)
  between operations  13.6 us (2%)
  starting transfers between devices  11 us (1%)
    all_to_all x1, blocking collectives, per_device(): lax.all_to_all(buffer, 'expert', split_axis=0, concat_axis=0, tiled=True)  288 us
    all_to_all x1, blocking collectives, per_device(): lax.all_to_all(jnp.stack([out_proj] * lax.axis_size('expert')), 'expert',...  199 us
    reduce_scatter x1, waiting for transfers between devices, per_device(): lax.psum_scatter(jnp.transpose(product_term, (3, 0, 1, 2, 4)).astype(jnp....  87.8 us
    all_to_all x1, waiting for transfers between devices, per_device(): lax.all_to_all(expert_out, 'expert', split_axis=0, concat_axis=0, tiled=T...  73.1 us
    another operation x3, other arithmetic  31.3 us
  transfers between devices with their start and end apart: 3, of which 3 were waited for; matrix products, arithmetic and copies ran while one was open for 5% of the time, Pallas kernels for 0%

profile of v1, /device:TPU:1, one launch (start us, length us, event | category | flops | bytes accessed | tf_op | source)
XLA Modules:
  0.0 799.5 jit_solution(13390582816836613498)
XLA Ops:
  6.5 2.1 stack.2
  8.7 199.2 %all_to_all.15 = bf16[64,1024,64]{1,2,0:T(8,128)(2,1)S(1)} all-to-all(bf16[64,1024,64]{1,2,0:T(8,128)(2,1)S(1)} %stack.2), channel_id=1, replica_groups=mesh['expert'=64,'tensor'=4] {'expert'}, dimensions={0} | all-to-all | bytes 16777216 | tf_op jit(solution)/shard_map/all_to_all | solution.py:34
  207.8 3.9 convolution_convert_fusion.1
  211.8 0.1 copy.48
  211.9 0.1 eq.43
  212.1 0.7 fusion.30
  212.8 31.1 %reduce-window.6 = s32[64,8,128]{2,1,0:T(8,128)S(1)} reduce-window(s32[64,8,128]{2,1,0:T(8,128)} %fusion.30, s32[]{:T(128)} %constant.11.clone.1), window={size=1x1x128 pad=0_0x0_0x127_0}, to_apply=%region_2.0 | reduce-window | flops 8323072 | bytes 524292 | tf_op jit(solution)/shard_map/reduce-window
  243.9 0.8 slice.10
  244.8 1.1 copy.50
  246.0 0.1 broadcast_add_fusion
  246.3 0.1 copy.53
  246.5 1.5 fusion.11
  247.9 10.0 %all-reduce.2.cloned.1.call-done = bf16[128,4096]{1,0:T(8,128)(2,1)} async-done(((bf16[128,4096]{1,0:T(8,128)(2,1)}), bf16[128,4096]{1,0:T(8,128)(2,1)}) %all-reduce.2.cloned.1.call-update) | async-done | bytes 1048592 | tf_op jit(solution)/shard_map/psum | solution.py:38
  257.9 3.4 convert_add_fusion
  261.3 5.1 convolution_convert_fusion
  266.5 13.9 %reshape.86 = bf16[64,1,18,4096]{3,2,0,1:T(8,128)(2,1)} reshape(bf16[1152,4096]{1,0:T(8,128)(2,1)} %convolution_convert_fusion) | data formatting | bytes 18874368 | tf_op jit(solution)/shard_map/reshape | solution.py:51
  280.4 288.3 %all_to_all.16 = bf16[64,1,18,4096]{3,2,1,0:T(8,128)(2,1)S(1)} all-to-all(bf16[64,1,18,4096]{3,2,1,0:T(8,128)(2,1)} %bitcast.99), channel_id=1, replica_groups=mesh['expert'=64,'tensor'=4] {'expert'}, dimensions={0} | all-to-all | bytes 18874368 | tf_op jit(solution)/shard_map/all_to_all | solution.py:52
  568.7 6.2 fusion.2
  574.9 7.3 fusion.20
  582.2 7.5 convert_bitcast_fusion
  589.7 9.0 %copy.75 = bf16[1,18,8,4,8,1024]{5,4,2,1,0,3:T(8,128)(2,1)} copy(bf16[1,18,8,4,8,1024]{5,4,3,2,1,0:T(8,128)(2,1)} %bitcast.102) | data formatting | bytes 18874368 | tf_op jit(solution)/shard_map/convert_element_type | solution.py:64
  598.7 87.8 %reduce-scatter.2.cloned.1.call-done = bf16[1,64,1,18,1024]{4,1,3,2,0:T(8,128)(2,1)} async-done(((bf16[4,64,1,18,1024]{4,1,3,2,0:T(8,128)(2,1)}), bf16[1,64,1,18,1024]{4,1,3,2,0:T(8,128)(2,1)}) %reduce-scatter.2.cloned.1.call-update) | async-done | bytes 2359312 | tf_op jit(solution)/shard_map/reduce_scatter | solution.py:63
  686.4 4.7 copy.57
  691.2 11.0 %all-to-all-start.2 = ((bf16[64,1,18,1024]{3,2,1,0:T(8,128)(2,1)}), bf16[64,1,18,1024]{3,2,1,0:T(8,128)(2,1)}, u32[]{:S(2)}, u32[]{:S(2)}) async-start(bf16[64,1,18,1024]{3,2,1,0:T(8,128)(2,1)} %copy.57), calls=%async_computation.3 | async-start | bytes 6291456 | tf_op jit(solution)/shard_map/all_to_all | solution.py:70
  702.1 0.1 copy.58
  702.2 0.1 reshape.95
  702.4 0.1 copy.47
  702.5 73.1 %all-to-all-done.2 = bf16[64,1,18,1024]{3,2,1,0:T(8,128)(2,1)} async-done(((bf16[64,1,18,1024]{3,2,1,0:T(8,128)(2,1)}), bf16[64,1,18,1024]{3,2,1,0:T(8,128)(2,1)}, u32[]{:S(2)}, u32[]{:S(2)}) %all-to-all-start.2) | async-done | bytes 2359328 | tf_op jit(solution)/shard_map/all_to_all | solution.py:70
  775.6 4.3 reshape.92
  779.9 8.0 %gather_fusion = bf16[1024,1024]{1,0:T(8,128)(2,1)} fusion(bf16[1152,1024]{1,0:T(8,128)(2,1)} %reshape.92, s32[1024]{0:T(1024)S(1)} %broadcast_clamp_fusion), kind=kCustom, calls=%fused_computation | custom fusion | bytes 4198400 | tf_op jit(solution)/shard_map/gather | solution.py:72
  787.9 2.9 fusion.7
  790.8 1.8 add_convert_fusion
  (34 shorter events, 0.6 us)
Async XLA Ops:
  6.5 575.7 %copy-start = (bf16[1,384,4096]{2,1,0:T(8,128)(2,1)S(1)}, bf16[1,384,4096]{2,1,0:T(8,128)(2,1)}, u32[]{:S(2)}) copy-start(bf16[1,384,4096]{2,1,0:T(8,128)(2,1)} %param.17) | copy-start | bytes 9437188
  6.5 251.4 %all-reduce.2.cloned.1.call-start = ((), (), s32[]{:S(2)}) async-start(), calls=%async_computation.4 | async-start | bytes 2097152 | tf_op jit(solution)/shard_map/psum | solution.py:38
  8.7 199.2 %copy-start.3 = (bf16[128,1024]{1,0:T(8,128)(2,1)S(1)}, bf16[128,1024]{1,0:T(8,128)(2,1)}, u32[]{:S(2)}) copy-start(bf16[128,1024]{1,0:T(8,128)(2,1)} %param.9) | copy-start | bytes 786436
  207.8 4.0 copy-start.5
  211.7 474.7 %reduce-scatter.2.cloned.1.call-start = ((), (), s32[]{:S(2)}) async-start(), calls=%async_computation.5 | async-start | bytes 11796480 | tf_op jit(solution)/shard_map/reduce_scatter | solution.py:63
  243.9 17.4 %copy-start.6 = (f32[4096]{0:T(1024)S(1)}, f32[4096]{0:T(1024)}, u32[]{:S(2)}) copy-start(f32[4096]{0:T(1024)} %param.12) | copy-start | bytes 49156
  257.9 3.4 copy-start.1
  257.9 3.4 copy-start.2
  280.4 288.3 %copy-start.7 = (bf16[1,4096,384]{2,1,0:T(8,128)(2,1)S(1)}, bf16[1,4096,384]{2,1,0:T(8,128)(2,1)}, u32[]{:S(2)}) copy-start(bf16[1,4096,384]{2,1,0:T(8,128)(2,1)} %param.15) | copy-start | bytes 9437188
  568.7 6.2 copy-start.8
  691.2 11.2 %copy-start.4 = (f32[128,8]{0,1:T(8,128)S(1)}, f32[128,8]{0,1:T(8,128)}, u32[]{:S(2)}) copy-start(f32[128,8]{0,1:T(8,128)} %param.14) | copy-start | bytes 12292
  691.2 84.4 %all-to-all-start.2 = ((bf16[64,1,18,1024]{3,2,1,0:T(8,128)(2,1)}), bf16[64,1,18,1024]{3,2,1,0:T(8,128)(2,1)}, u32[]{:S(2)}, u32[]{:S(2)}) async-start(bf16[64,1,18,1024]{3,2,1,0:T(8,128)(2,1)} %copy.57), calls=%async_computation.3 | async-start | bytes 6291456 | tf_op jit(solution)/shard_map/all_to_all | solution.py:70
Sparse Core Ops, SparseCore 0:
  211.9 45.9 all-reduce.1
  598.8 87.5 reduce-scatter.1
